TPU v7x, 32 devices: a whole 2x2x4 slice. The times are simulated.
32 devices in a mesh: row: 8 (over z, core), aux: 4 (over y, x).
Axes of the slice: x: 2, y: 2, z: 4, core: 2. Of those that a mesh axis runs over, the one named last changes fastest.
Arguments:
- factor_ia: float32 [64, 12288], P('row', 'aux'), may hold values from -0.8 to 0.8
- factor_jb: float32 [5120, 12288], P('row', 'aux'), may hold values from -0.8 to 0.8
- denominators: float32 [64, 5120], P(None, 'row'), may hold values from 0.5 to 8
Outputs:
- grad_jb: float32 [5120, 12288], P('row', 'aux')
- grad_ia: float32 [64, 12288], P('row', 'aux')
All inputs are finite; a program needn't handle non-finite values.
Results may differ from a plain program's by a relative error of at most 0.00011.
Values sent between devices are 32-bit elements; how exact they have to be, the bound alone decides.
No kernel may reach another device: no remote copies, remote signals or barrier semaphores. Data moves between devices by JAX's collectives and lax.ppermute only.
A program may use at most 64 MiB of HBM per device.

v0:
```python
import jax
import jax.numpy as jnp
from jax import lax
from jax.sharding import PartitionSpec as P


def per_device(factor_ia, factor_jb, denominators):
    whole_ia = lax.all_gather(factor_ia, "row", axis=0, tiled=True)
    partial_value = lax.dot_general(
        whole_ia,
        factor_jb,
        (((1,), (1,)), ((), ())),
        precision=lax.Precision.HIGHEST,
        preferred_element_type=jnp.float32,
    )
    share_width = denominators.shape[1] // lax.axis_size("aux")
    share_start = lax.axis_index("aux") * share_width
    integral_part = lax.psum_scatter(partial_value, "aux", scatter_dimension=1, tiled=True)
    denom_part = lax.dynamic_slice_in_dim(denominators, share_start, share_width, 1)
    amplitudes = lax.all_gather(integral_part / denom_part, "aux", axis=1, tiled=True)
    grad_jb = lax.dot_general(
        amplitudes,
        whole_ia,
        (((0,), (0,)), ((), ())),
        precision=lax.Precision.HIGHEST,
        preferred_element_type=jnp.float32,
    )
    grad_ia = lax.psum_scatter(
        jnp.dot(
            amplitudes,
            factor_jb,
            precision=lax.Precision.HIGHEST,
            preferred_element_type=jnp.float32,
        ),
        "row",
        scatter_dimension=0,
        tiled=True,
    )
    return (grad_jb, grad_ia)


def solution(mesh):
    return jax.shard_map(
        per_device,
        mesh=mesh,
        in_specs=(P("row", "aux"), P("row", "aux"), P(None, "row")),
        out_specs=(P("row", "aux"), P("row", "aux")),
        check_vma=False,
    )
```

profile of v0, /device:TPU:0, one launch (start us, length us, event | category | flops | bytes accessed | tf_op | source)
XLA Modules:
  0.0 119.1 jit_solution(13380019254326274909)
XLA Ops:
  7.2 0.0 reduce-scatter.7.cloned.1.call-start
  7.2 17.4 %all_gather.6 = f32[64,3072]{1,0:T(8,128)S(1)} all-gather(f32[8,3072]{1,0:T(8,128)} %param.3), channel_id=1, replica_groups=mesh['row'=8,'aux'=4] {'row'}, dimensions={0}, use_global_device_ids=true | all-gather | bytes 884736 | tf_op jit(solution)/shard_map/all_gather | solution.py:8
  24.6 9.2 %convolution_bitcast_fusion = f32[640,64]{1,0:T(8,128)} fusion(f32[64,3072]{1,0:T(8,128)S(1)} %all_gather.6, f32[640,3072]{1,0:T(8,128)} %param.4), kind=kOutput, calls=%fused_computation | convolution fusion | flops 1509949440 | bytes 8814592
  33.8 0.0 reduce-scatter.7.cloned.1.call-update
  33.8 0.0 reduce-scatter.5.cloned.1.call-start
  33.9 25.8 %reduce-scatter.7.cloned.1.call-done = f32[160,64]{1,0:T(8,128)} async-done(((f32[640,64]{1,0:T(8,128)}), f32[160,64]{1,0:T(8,128)}) %reduce-scatter.7.cloned.1.call-update) | async-done | bytes 40976
  59.7 1.0 copy.8
  60.6 1.0 divide_bitcast_fusion
  61.6 9.3 %all-gather = f32[4,160,64]{1,2,0:T(8,128)S(1)} all-gather(f32[1,160,64]{1,2,0:T(8,128)S(1)} %divide_bitcast_fusion), channel_id=1, replica_groups=mesh['row'=8,'aux'=4] {'aux'}, dimensions={0}, use_global_device_ids=true | all-gather | bytes 204800 | tf_op jit(solution)/shard_map/all_gather | solution.py:20
  70.9 0.2 copy.6
  71.1 0.2 reshape.5
  71.3 8.9 %fusion.1 = f32[64,3072]{1,0:T(8,128)} fusion(f32[640,64]{0,1:T(8,128)S(1)} %reshape.5, f32[640,3072]{1,0:T(8,128)} %param.4), kind=kOutput, calls=%fused_computation.3 | convolution fusion | flops 1509949440 | bytes 8814592 | tf_op jit(solution)/shard_map/dot_general | solution.py:29
  80.2 0.0 reduce-scatter.5.cloned.1.call-update
  80.2 8.5 %fusion = f32[640,3072]{1,0:T(8,128)} fusion(f32[640,64]{0,1:T(8,128)S(1)} %reshape.5, f32[64,3072]{1,0:T(8,128)S(1)} %all_gather.6), kind=kOutput, calls=%fused_computation.2 | convolution fusion | flops 1509949440 | bytes 8814592 | tf_op jit(solution)/shard_map/dot_general | solution.py:21
  88.7 23.5 %reduce-scatter.5.cloned.1.call-done = f32[8,3072]{1,0:T(8,128)} async-done(((f32[64,3072]{1,0:T(8,128)}), f32[8,3072]{1,0:T(8,128)}) %reduce-scatter.5.cloned.1.call-update) | async-done | bytes 98320 | tf_op jit(solution)/shard_map/reduce_scatter | solution.py:28
Async XLA Ops:
  7.2 52.5 %reduce-scatter.7.cloned.1.call-start = ((), (), s32[]{:S(2)}) async-start(), calls=%async_computation.3 | async-start | bytes 409600
  33.8 78.4 %reduce-scatter.5.cloned.1.call-start = ((), (), s32[]{:S(2)}) async-start(), calls=%async_computation.2 | async-start | bytes 884736 | tf_op jit(solution)/shard_map/reduce_scatter | solution.py:28
Sparse Core Ops, SparseCore 0:
  34.0 25.6 reduce-scatter.6
  80.4 31.8 reduce-scatter.4
where the time goes:
time: 119 us
  waiting for transfers between devices  49.3 us (41%)
  blocking collectives  26.7 us (22%)
  matrix products  26.6 us (22%)
  between operations  14.1 us (12%)
  local copies, waits for them, and re-layouts  1.31 us (1%)
    unnamed x3, waiting for transfers between devices  25.8 us
    reduce_scatter x1, waiting for transfers between devices, per_device(): lax.psum_scatter(jnp.dot(amplitudes, factor_jb, precision=lax.Precision.H...  23.5 us
    all_gather x1, blocking collectives, per_device(): whole_ia = lax.all_gather(factor_ia, 'row', axis=0, tiled=True)  17.4 us
    all_gather x1, blocking collectives, per_device(): lax.all_gather(integral_part / denom_part, 'aux', axis=1, tiled=True)  9.29 us
    unnamed x1, matrix products  9.18 us
    dot_general x1, matrix products, per_device(): jnp.dot(amplitudes, factor_jb, precision=lax.Precision.HIGHEST, preferred...  8.92 us
    dot_general x1, matrix products, per_device(): lax.dot_general(amplitudes, whole_ia, (((0,), (0,)), ((), ())), precision...  8.48 us
  transfers between devices with their start and end apart: 2, of which 2 were waited for; matrix products, arithmetic and copies ran while one was open for 7% of the time, Pallas kernels for 0%

commit v1 on v0

--- a/solution.py
+++ b/solution.py
@@ -1,11 +1,31 @@
+import functools
 import jax
 import jax.numpy as jnp
 from jax import lax
 from jax.sharding import PartitionSpec as P
 
 
+def bands_store(target, bus_axis):
+    samples = []
+    p_count = lax.axis_size(bus_axis)
+    for w in tuple(range(1, p_count)):
+        samples.append((w - 1, w))
+    current_block = target
+    part_now = samples + [(p_count - 1, 0)]
+    grid = [current_block]
+    for _ in [*range(p_count - 1)]:
+        current_block = lax.ppermute(current_block, bus_axis, part_now)
+        grid += [current_block]
+    work_now = jnp.concatenate([*reversed(grid)], 0)
+    row_out = lax.axis_index(bus_axis)
+    return jnp.roll(work_now, (row_out + 1) * current_block.shape[0], 0)
+
+
+end_run = functools.partial(bands_store, bus_axis="row")
+
+
 def per_device(factor_ia, factor_jb, denominators):
-    whole_ia = lax.all_gather(factor_ia, "row", axis=0, tiled=True)
+    whole_ia = end_run(factor_ia)
     partial_value = lax.dot_general(
         whole_ia,
         factor_jb,

time: 119 us -> 143 us (1.20)
  waiting for transfers between devices: 49.3 us -> 88.5 us
  blocking collectives: 26.7 us -> 9.45 us
    ppermute x0 -> x7, waiting for transfers between devices: none -> 41.6 us  [bands_store(): current_block = lax.ppermute(current_block, bus_axis, part_now)]
    all_gather x1 -> x0, blocking collectives: 17.4 us -> none  [per_device(): whole_ia = lax.all_gather(factor_ia, 'row', axis=0, tiled=True)]
    unnamed x3, waiting for transfers between devices: 25.8 us -> 23.4 us
  transfers between devices with their start and end apart: 2 -> 9, of which waited for: 2 -> 9; matrix products, arithmetic and copies ran while one was open for 7% -> 6% of each run, Pallas kernels for 0% -> 0%
where the time goes in v1:
time: 143 us
  waiting for transfers between devices  88.5 us (62%)
  matrix products  26.6 us (19%)
  between operations  14.2 us (10%)
  blocking collectives  9.45 us (7%)
  local copies, waits for them, and re-layouts  2.36 us (2%)
    ppermute x7, waiting for transfers between devices, bands_store(): current_block = lax.ppermute(current_block, bus_axis, part_now)  41.6 us
    reduce_scatter x1, waiting for transfers between devices, per_device(): lax.psum_scatter(jnp.dot(amplitudes, factor_jb, precision=lax.Precision.H...  23.6 us
    unnamed x3, waiting for transfers between devices  23.4 us
    all_gather x1, blocking collectives, per_device(): lax.all_gather(integral_part / denom_part, 'aux', axis=1, tiled=True)  9.45 us
    unnamed x1, matrix products  9.21 us
    dot_general x1, matrix products, per_device(): jnp.dot(amplitudes, factor_jb, precision=lax.Precision.HIGHEST, preferred...  8.92 us
    dot_general x1, matrix products, per_device(): lax.dot_general(amplitudes, whole_ia, (((0,), (0,)), ((), ())), precision...  8.49 us
  transfers between devices with their start and end apart: 9, of which 9 were waited for; matrix products, arithmetic and copies ran while one was open for 6% of the time, Pallas kernels for 0%

profile of v1, /device:TPU:0, one launch (start us, length us, event | category | flops | bytes accessed | tf_op | source)
XLA Modules:
  0.0 142.8 jit_solution(9023773519183549174)
XLA Ops:
  7.2 0.0 copy-start
  7.2 0.0 reduce-scatter.7.cloned.1.call-start
  7.2 0.5 collective-permute-start
  7.8 6.5 %collective-permute-done = f32[8,3072]{1,0:T(8,128)S(1)} collective-permute-done((f32[8,3072]{1,0:T(8,128)}, f32[8,3072]{1,0:T(8,128)S(1)}, u32[]{:S(2)}, u32[]{:S(2)}) %collective-permute-start) | collective-permute-done | bytes 98336 | tf_op jit(solution)/shard_map/ppermute | solution.py:17
  14.3 0.0 collective-permute-start.1
  14.3 5.8 %collective-permute-done.1 = f32[8,3072]{1,0:T(8,128)S(1)} collective-permute-done((f32[8,3072]{1,0:T(8,128)S(1)}, f32[8,3072]{1,0:T(8,128)S(1)}, u32[]{:S(2)}, u32[]{:S(2)}) %collective-permute-start.1) | collective-permute-done | bytes 98336 | tf_op jit(solution)/shard_map/ppermute | solution.py:17
  20.1 0.0 collective-permute-start.2
  20.1 5.8 %collective-permute-done.2 = f32[8,3072]{1,0:T(8,128)S(1)} collective-permute-done((f32[8,3072]{1,0:T(8,128)S(1)}, f32[8,3072]{1,0:T(8,128)S(1)}, u32[]{:S(2)}, u32[]{:S(2)}) %collective-permute-start.2) | collective-permute-done | bytes 98336 | tf_op jit(solution)/shard_map/ppermute | solution.py:17
  26.0 0.0 collective-permute-start.3
  26.0 5.8 %collective-permute-done.3 = f32[8,3072]{1,0:T(8,128)S(1)} collective-permute-done((f32[8,3072]{1,0:T(8,128)S(1)}, f32[8,3072]{1,0:T(8,128)S(1)}, u32[]{:S(2)}, u32[]{:S(2)}) %collective-permute-start.3) | collective-permute-done | bytes 98336 | tf_op jit(solution)/shard_map/ppermute | solution.py:17
  31.8 0.0 collective-permute-start.4
  31.8 5.8 %collective-permute-done.4 = f32[8,3072]{1,0:T(8,128)S(1)} collective-permute-done((f32[8,3072]{1,0:T(8,128)S(1)}, f32[8,3072]{1,0:T(8,128)S(1)}, u32[]{:S(2)}, u32[]{:S(2)}) %collective-permute-start.4) | collective-permute-done | bytes 98336 | tf_op jit(solution)/shard_map/ppermute | solution.py:17
  37.7 0.0 collective-permute-start.5
  37.7 5.8 %collective-permute-done.5 = f32[8,3072]{1,0:T(8,128)S(1)} collective-permute-done((f32[8,3072]{1,0:T(8,128)S(1)}, f32[8,3072]{1,0:T(8,128)S(1)}, u32[]{:S(2)}, u32[]{:S(2)}) %collective-permute-start.5) | collective-permute-done | bytes 98336 | tf_op jit(solution)/shard_map/ppermute | solution.py:17
  43.5 0.0 collective-permute-start.6
  43.5 5.8 %collective-permute-done.6 = f32[8,3072]{1,0:T(8,128)S(1)} collective-permute-done((f32[8,3072]{1,0:T(8,128)S(1)}, f32[8,3072]{1,0:T(8,128)S(1)}, u32[]{:S(2)}, u32[]{:S(2)}) %collective-permute-start.6) | collective-permute-done | bytes 98336 | tf_op jit(solution)/shard_map/ppermute | solution.py:17
  49.5 0.9 constant_dynamic-update-slice_fusion.8
  50.5 0.0 copy-done
  50.5 9.2 %convolution_bitcast_fusion = f32[640,64]{1,0:T(8,128)} fusion(f32[640,3072]{1,0:T(8,128)} %param.4, f32[128,3072]{1,0:T(8,128)S(1)} %constant_dynamic-update-slice_fusion, s32[]{:T(128)S(6)} %select_n.17), kind=kOutput, calls=%fused_computation | convolution fusion | flops 1509949440 | bytes 8814596
  59.7 0.0 reduce-scatter.7.cloned.1.call-update
  59.7 0.0 reduce-scatter.5.cloned.1.call-start
  59.8 23.3 %reduce-scatter.7.cloned.1.call-done = f32[160,64]{1,0:T(8,128)} async-done(((f32[640,64]{1,0:T(8,128)}), f32[160,64]{1,0:T(8,128)}) %reduce-scatter.7.cloned.1.call-update) | async-done | bytes 40976
  83.1 1.0 copy.8
  84.1 1.0 divide_bitcast_fusion
  85.1 9.5 %all-gather = f32[4,160,64]{1,2,0:T(8,128)S(1)} all-gather(f32[1,160,64]{1,2,0:T(8,128)S(1)} %divide_bitcast_fusion), channel_id=1, replica_groups=mesh['row'=8,'aux'=4] {'aux'}, dimensions={0}, use_global_device_ids=true | all-gather | bytes 204800 | tf_op jit(solution)/shard_map/all_gather | solution.py:40
  94.6 0.2 copy.6
  94.7 0.2 reshape.5
  94.9 8.9 %fusion.5 = f32[64,3072]{1,0:T(8,128)} fusion(f32[640,64]{0,1:T(8,128)S(1)} %reshape.5, f32[640,3072]{1,0:T(8,128)} %param.4), kind=kOutput, calls=%fused_computation.23 | convolution fusion | flops 1509949440 | bytes 8814592 | tf_op jit(solution)/shard_map/dot_general | solution.py:49
  103.8 0.0 reduce-scatter.5.cloned.1.call-update
  103.9 8.5 %fusion = f32[640,3072]{1,0:T(8,128)} fusion(f32[640,64]{0,1:T(8,128)S(1)} %reshape.5, f32[128,3072]{1,0:T(8,128)S(1)} %constant_dynamic-update-slice_fusion, s32[]{:T(128)S(6)} %select_n.17), kind=kOutput, calls=%fused_computation.1 | convolution fusion | flops 1509949440 | bytes 8814596 | tf_op jit(solution)/shard_map/dot_general | solution.py:41
  112.3 23.6 %reduce-scatter.5.cloned.1.call-done = f32[8,3072]{1,0:T(8,128)} async-done(((f32[64,3072]{1,0:T(8,128)}), f32[8,3072]{1,0:T(8,128)}) %reduce-scatter.5.cloned.1.call-update) | async-done | bytes 98320 | tf_op jit(solution)/shard_map/reduce_scatter | solution.py:48
  (15 shorter events, 0.1 us)
Async XLA Ops:
  7.2 43.3 %copy-start = (f32[8,3072]{1,0:T(8,128)S(1)}, f32[8,3072]{1,0:T(8,128)}, u32[]{:S(2)}) copy-start(f32[8,3072]{1,0:T(8,128)} %param.3) | copy-start | bytes 294916
  7.2 76.0 %reduce-scatter.7.cloned.1.call-start = ((), (), s32[]{:S(2)}) async-start(), calls=%async_computation.3 | async-start | bytes 409600
  7.2 7.1 %collective-permute-start = (f32[8,3072]{1,0:T(8,128)}, f32[8,3072]{1,0:T(8,128)S(1)}, u32[]{:S(2)}, u32[]{:S(2)}) collective-permute-start(f32[8,3072]{1,0:T(8,128)} %param.3), channel_id=1, source_target_pairs={{0,4},{4,8},{8,12},{12,16},{16,20},{20,24},{24,28},{28,0},{1,5},{5... | collective-permute-start | bytes 294920 | tf_op jit(solution)/shard_map/ppermute | solution.py:17
  14.3 5.8 %collective-permute-start.1 = (f32[8,3072]{1,0:T(8,128)S(1)}, f32[8,3072]{1,0:T(8,128)S(1)}, u32[]{:S(2)}, u32[]{:S(2)}) collective-permute-start(f32[8,3072]{1,0:T(8,128)S(1)} %collective-permute-done), channel_id=1, source_target_pairs={{0,4},{4,8},{8,12},{12,16},{16,20},{20,24},{24,28},{28,0},{1,5},{5... | collective-permute-start | bytes 294920 | tf_op jit(solution)/shard_map/ppermute | solution.py:17
  20.1 5.8 %collective-permute-start.2 = (f32[8,3072]{1,0:T(8,128)S(1)}, f32[8,3072]{1,0:T(8,128)S(1)}, u32[]{:S(2)}, u32[]{:S(2)}) collective-permute-start(f32[8,3072]{1,0:T(8,128)S(1)} %collective-permute-done.1), channel_id=1, source_target_pairs={{0,4},{4,8},{8,12},{12,16},{16,20},{20,24},{24,28},{28,0},{1,5},{5... | collective-permute-start | bytes 294920 | tf_op jit(solution)/shard_map/ppermute | solution.py:17
  26.0 5.8 %collective-permute-start.3 = (f32[8,3072]{1,0:T(8,128)S(1)}, f32[8,3072]{1,0:T(8,128)S(1)}, u32[]{:S(2)}, u32[]{:S(2)}) collective-permute-start(f32[8,3072]{1,0:T(8,128)S(1)} %collective-permute-done.2), channel_id=1, source_target_pairs={{0,4},{4,8},{8,12},{12,16},{16,20},{20,24},{24,28},{28,0},{1,5},{5... | collective-permute-start | bytes 294920 | tf_op jit(solution)/shard_map/ppermute | solution.py:17
  31.8 5.8 %collective-permute-start.4 = (f32[8,3072]{1,0:T(8,128)S(1)}, f32[8,3072]{1,0:T(8,128)S(1)}, u32[]{:S(2)}, u32[]{:S(2)}) collective-permute-start(f32[8,3072]{1,0:T(8,128)S(1)} %collective-permute-done.3), channel_id=1, source_target_pairs={{0,4},{4,8},{8,12},{12,16},{16,20},{20,24},{24,28},{28,0},{1,5},{5... | collective-permute-start | bytes 294920 | tf_op jit(solution)/shard_map/ppermute | solution.py:17
  37.7 5.8 %collective-permute-start.5 = (f32[8,3072]{1,0:T(8,128)S(1)}, f32[8,3072]{1,0:T(8,128)S(1)}, u32[]{:S(2)}, u32[]{:S(2)}) collective-permute-start(f32[8,3072]{1,0:T(8,128)S(1)} %collective-permute-done.4), channel_id=1, source_target_pairs={{0,4},{4,8},{8,12},{12,16},{16,20},{20,24},{24,28},{28,0},{1,5},{5... | collective-permute-start | bytes 294920 | tf_op jit(solution)/shard_map/ppermute | solution.py:17
  43.5 5.8 %collective-permute-start.6 = (f32[8,3072]{1,0:T(8,128)S(1)}, f32[8,3072]{1,0:T(8,128)S(1)}, u32[]{:S(2)}, u32[]{:S(2)}) collective-permute-start(f32[8,3072]{1,0:T(8,128)S(1)} %collective-permute-done.5), channel_id=1, source_target_pairs={{0,4},{4,8},{8,12},{12,16},{16,20},{20,24},{24,28},{28,0},{1,5},{5... | collective-permute-start | bytes 294920 | tf_op jit(solution)/shard_map/ppermute | solution.py:17
  59.7 76.2 %reduce-scatter.5.cloned.1.call-start = ((), (), s32[]{:S(2)}) async-start(), calls=%async_computation.2 | async-start | bytes 884736 | tf_op jit(solution)/shard_map/reduce_scatter | solution.py:48
Sparse Core Ops, SparseCore 0:
  59.9 23.2 reduce-scatter.6
  104.0 31.9 reduce-scatter.4
